TPU v7x, 256 devices: a whole 4x4x8 slice. The times are simulated.
256 devices in a mesh: head: 8 (over y, core), tok: 32 (over x, z).
Axes of the slice: x: 4, y: 4, z: 8, core: 2. Of those that a mesh axis runs over, the one named last changes fastest.
Arguments:
- queries: bfloat16 [32768, 4096], P('tok', 'head'), may hold values from -100 to 100
- keys: bfloat16 [32768, 4096], P('tok', 'head'), may hold values from -6 to 6
- values: bfloat16 [32768, 4096], P('tok', 'head'), may hold values from -6 to 6
- step_size: float32 [32768, 8], P('tok', 'head'), may hold values from 6.1035156e-05 to 0.00061035156
- fast_one: bfloat16 [8, 512, 512], P('head'), may hold values from -0.25 to 0.25
- fast_three: bfloat16 [8, 512, 512], P('head'), may hold values from -0.25 to 0.25
- fast_two: bfloat16 [8, 512, 512], P('head'), may hold values from -0.25 to 0.25
- out_proj: bfloat16 [4096, 4096], P('tok', 'head'), may hold values from -0.09375 to 0.09375
- view_units: int32 [64], replicated, may hold values from 1 to 8, 256 in all
- evening: int32 [32, 32], P('tok'), may hold values from 0 to 31, each once within a row
Outputs:
- evened: bfloat16 [32768, 4096], P('tok', 'head')
Inputs may be any that keep to these rules, and one draw needn't show every extreme that they name: `view_units`: the lengths sum to 256; the longest is exactly 8. `evening`: each row is a permutation of the token shards.
All inputs are finite; a program needn't handle non-finite values.
Results may differ from a plain program's by a relative error of at most 0.01.
The roundings to bfloat16 on the way count: a program that leaves them out, or rounds other values in their place, can miss the bound.
Values may be sent and summed in bfloat16 or wider, within the bound.
No kernel may reach another device: no remote copies, remote signals or barrier semaphores. Data moves between devices by JAX's collectives and lax.ppermute only.
A program may use at most 64 MiB of HBM per device.

v0:
```python
import jax
import jax.numpy as jnp
from jax import lax
from jax.sharding import PartitionSpec as P

DH = 512
VIEW_UNIT = 128
VIEW_MOST = 8


def from_behind(value, axis, steps):
    count = lax.axis_size(axis)
    leading, last = (max(0, -steps), min(count, count - steps))
    return lax.ppermute(value, axis, [(source, source + steps) for source in range(leading, last)])


def view_lookup(view_units, positions, total_tokens):
    view_ends = jnp.cumsum(view_units) * VIEW_UNIT
    inside = (positions >= 0) & (positions < total_tokens)
    labels = jnp.sum((positions[:, None] >= view_ends[None, :]).astype(jnp.int32), axis=1)
    return jnp.where(inside, labels, -1)


def rms_rows(rows):
    return rows * lax.rsqrt(jnp.mean(rows * rows, axis=-1, keepdims=True) + 1e-06)


def local(
    queries, keys, values, step_size, fast_one, fast_three, fast_two, out_proj, view_units, evening
):
    shard_count = lax.axis_size("tok")
    my_shard = lax.axis_index("tok")
    tok_dev = queries.shape[0]
    local_width = queries.shape[1]
    heads_here = local_width // DH
    total_tokens = tok_dev * shard_count
    reach_span = (VIEW_MOST * VIEW_UNIT + tok_dev - 2) // tok_dev
    scale = DH ** (-0.5)
    local_rows = jnp.arange(tok_dev, dtype=jnp.int32)
    stacked = jnp.stack([keys, values])
    pieces = []
    labels = []
    offsets = list(range(reach_span, 0, -1)) + [0] + list(range(-1, -reach_span - 1, -1))
    for offset in offsets:
        if offset == 0:
            pieces.append(stacked)
        else:
            pieces.append(from_behind(stacked, "tok", offset))
        labels.append(
            view_lookup(view_units, (my_shard - offset) * tok_dev + local_rows, total_tokens)
        )
    window = jnp.concatenate(pieces, axis=1)
    key_views = jnp.concatenate(labels)
    key_heads = window[0].reshape(-1, heads_here, DH)
    value_heads = window[1].reshape(-1, heads_here, DH)
    window_rows = key_heads.shape[0]
    query_views = view_lookup(view_units, my_shard * tok_dev + local_rows, total_tokens)
    block_rows = min(512, tok_dev)
    n_blocks = tok_dev // block_rows
    key_span = min(window_rows, block_rows + 2 * VIEW_MOST * VIEW_UNIT)
    lead_shift = reach_span * tok_dev - VIEW_MOST * VIEW_UNIT

    def attend(block_index):
        start = block_index * block_rows
        key_start = jnp.clip(start + lead_shift, 0, window_rows - key_span)
        query_rows = lax.dynamic_slice_in_dim(queries, start, block_rows, 0).reshape(
            block_rows, heads_here, DH
        )
        row_views = lax.dynamic_slice_in_dim(query_views, start, block_rows, 0)
        near_keys = lax.dynamic_slice_in_dim(key_heads, key_start, key_span, 0)
        near_values = lax.dynamic_slice_in_dim(value_heads, key_start, key_span, 0)
        near_views = lax.dynamic_slice_in_dim(key_views, key_start, key_span, 0)
        scores = (
            jnp.einsum("qhd,khd->hqk", query_rows, near_keys, preferred_element_type=jnp.float32)
            * scale
        )
        same_view = row_views[:, None] == near_views[None, :]
        scores = jnp.where(same_view[None], scores, -1e30)
        top = jnp.max(scores, axis=-1, keepdims=True)
        weights = jnp.exp(scores - top)
        probs = (weights / jnp.sum(weights, axis=-1, keepdims=True)).astype(jnp.bfloat16)
        out_rows = jnp.einsum(
            "hqk,khd->qhd", probs, near_values, preferred_element_type=jnp.float32
        )
        return out_rows.reshape(block_rows, local_width)

    attended = lax.map(attend, jnp.arange(n_blocks, dtype=jnp.int32)).reshape(tok_dev, local_width)
    query_norm = rms_rows(queries.reshape(tok_dev, heads_here, DH).astype(jnp.float32)).astype(
        jnp.bfloat16
    )
    key_norm = rms_rows(keys.reshape(tok_dev, heads_here, DH).astype(jnp.float32)).astype(
        jnp.bfloat16
    )
    gate_pre = jnp.einsum("thd,hdf->htf", key_norm, fast_one, preferred_element_type=jnp.float32)
    up_pre = jnp.einsum("thd,hdf->htf", key_norm, fast_three, preferred_element_type=jnp.float32)
    gate_sig = jax.nn.sigmoid(gate_pre)
    hidden_keys = (gate_pre * gate_sig * up_pre).astype(jnp.bfloat16)
    descent = (
        -step_size[:, :, None] * values.reshape(tok_dev, heads_here, DH).astype(jnp.float32)
    ).astype(jnp.bfloat16)
    grad_two = jnp.einsum("htf,thd->hfd", hidden_keys, descent, preferred_element_type=jnp.float32)
    back = jnp.einsum("thd,hfd->htf", descent, fast_two, preferred_element_type=jnp.float32)
    grad_gate = (back * up_pre * gate_sig * (1.0 + gate_pre * (1.0 - gate_sig))).astype(
        jnp.bfloat16
    )
    grad_up = (back * gate_pre * gate_sig).astype(jnp.bfloat16)
    grad_one = jnp.einsum("thd,htf->hdf", key_norm, grad_gate, preferred_element_type=jnp.float32)
    grad_three = jnp.einsum("thd,htf->hdf", key_norm, grad_up, preferred_element_type=jnp.float32)
    total_one, total_three, total_two = lax.psum((grad_one, grad_three, grad_two), "tok")
    new_one = (fast_one.astype(jnp.float32) - total_one).astype(jnp.bfloat16)
    new_three = (fast_three.astype(jnp.float32) - total_three).astype(jnp.bfloat16)
    new_two = (fast_two.astype(jnp.float32) - total_two).astype(jnp.bfloat16)
    gate_q = jnp.einsum("thd,hdf->htf", query_norm, new_one, preferred_element_type=jnp.float32)
    up_q = jnp.einsum("thd,hdf->htf", query_norm, new_three, preferred_element_type=jnp.float32)
    hidden_q = (gate_q * jax.nn.sigmoid(gate_q) * up_q).astype(jnp.bfloat16)
    fast_out = jnp.einsum(
        "htf,hfd->thd", hidden_q, new_two, preferred_element_type=jnp.float32
    ).reshape(tok_dev, local_width)
    mixed = (attended + fast_out).astype(jnp.bfloat16)
    mixed_full = lax.all_gather(mixed, "head", axis=1, tiled=True)
    projected = jnp.dot(
        mixed_full,
        lax.all_gather(out_proj, "tok", axis=0, tiled=True),
        preferred_element_type=jnp.float32,
    ).astype(jnp.bfloat16)
    tiles = projected.reshape(shard_count, tok_dev // shard_count, out_proj.shape[1])
    targets = evening.reshape(shard_count)
    match = (targets[None, :] == jnp.arange(shard_count, dtype=jnp.int32)[:, None]).astype(
        jnp.int32
    )
    order_index = jnp.argmax(match, axis=1)
    outgoing = tiles[order_index]
    arrived = lax.all_to_all(outgoing, "tok", split_axis=0, concat_axis=0, tiled=True)
    return arrived.reshape(tok_dev, out_proj.shape[1])


def solution(mesh):
    return jax.shard_map(
        local,
        mesh=mesh,
        in_specs=(
            P("tok", "head"),
            P("tok", "head"),
            P("tok", "head"),
            P("tok", "head"),
            P("head", None, None),
            P("head", None, None),
            P("head", None, None),
            P("tok", "head"),
            P(),
            P("tok", None),
        ),
        out_specs=P("tok", "head"),
        check_vma=False,
    )
```

profile of v0, /device:TPU:32, one launch (start us, length us, event | category | flops | bytes accessed | tf_op | source)
XLA Modules:
  0.0 387.9 jit_solution(13279123578200900547)
XLA Ops:
  6.5 0.0 all-reduce.3.cloned.1.call-start
  6.5 1.5 fusion.12
  8.0 0.0 copy-start
  8.1 0.0 copy-start.5
  8.1 2.2 fusion.30
  10.3 0.0 copy-start.6
  10.3 0.0 copy-start.1
  10.4 0.0 copy-start.4
  10.4 0.8 fusion.28
  11.2 0.4 copy-done.1
  11.6 0.1 copy-done.4
  11.7 0.8 fusion.26
  12.5 2.1 convolution_bitcast_fusion
  14.6 2.3 convolution_bitcast_fusion.1
  16.9 2.1 convolution_bitcast_fusion.2
  19.0 0.0 all-reduce.3.cloned.1.call-update
  19.0 0.0 all-gather.5.cloned.1.call-start
  19.0 0.7 all-gather.5.cloned.1.call-update
  19.7 0.0 all-gather.3.cloned.1.call-start
  19.8 0.0 copy-start.7
  19.8 0.0 copy-start.2
  19.8 1.5 pad_maximum_fusion.1
  21.3 3.8 collective-permute-start
  25.2 3.5 collective-permute-start.1
  28.7 0.1 copy.15
  28.8 0.1 reduce-window.8
  28.9 0.1 multiply_reduce_fusion
  29.1 0.2 convert_reduce_fusion.1
  29.3 0.3 fusion.14
  29.6 61.3 %collective-permute-done = bf16[2,1024,512]{2,1,0:T(8,128)(2,1)} collective-permute-done((bf16[2,1024,512]{2,1,0:T(8,128)(2,1)}, bf16[2,1024,512]{2,1,0:T(8,128)(2,1)}, u32[]{:S(2)}, u32[]{:S(2)}) %collective-permute-start) | collective-permute-done | bytes 2097184 | tf_op jit(solution)/shard_map/ppermute | solution.py:14
  90.9 4.1 %collective-permute-done.1 = bf16[2,1024,512]{2,1,0:T(8,128)(2,1)} collective-permute-done((bf16[2,1024,512]{2,1,0:T(8,128)(2,1)}, bf16[2,1024,512]{2,1,0:T(8,128)(2,1)}, u32[]{:S(2)}, u32[]{:S(2)}) %collective-permute-start.1) | collective-permute-done | bytes 2097184 | tf_op jit(solution)/shard_map/ppermute | solution.py:14
  95.1 3.5 pad_maximum_fusion
  98.6 3.1 slice_bitcast_fusion
  101.6 58.6 %while.10 = (s32[]{:T(128)}, f32[2,512,512]{1,0,2:T(2,128)}, s32[2]{0:T(128)S(1)}, bf16[3072,1,512]{2,0,1:T(8,128)(2,1)}, s32[1024]{0:T(1024)S(1)}, /*index=5*/s...) while((s32[]{:T(128)}, f32[2,512,512]{1,0,2:T(2,128)}, ...), condition=%wide.region_7.8_spmd, body=%wide.region_4.7_spmd.sunk | while | flops 2696150016 | bytes 39371012 | solution.py:87
  101.6 0.7 dynamic_slice.44
  103.0 0.1 dynamic_slice.46
  103.1 0.1 dynamic_slice.45
  103.2 3.6 fusion.51
  106.8 0.8 fusion.52
  107.6 1.1 copy-done.3
  108.7 1.8 fusion.53
  110.5 1.1 copy.23
  111.6 19.4 %dynamic_update_slice.5 = f32[2,512,512]{1,0,2:T(2,128)} dynamic-update-slice(f32[2,512,512]{1,0,2:T(2,128)} %get-tuple-element.145, f32[1,512,512]{1,0,2:T(1,128)S(1)} %copy.23, s32[]{:T(128)} %get-tuple-element.144, s32[]{:T(128)} %constant.16.clone.1..sunk, s32[]{:T(128)} %constant.16.clone.1..sunk) | dynamic-update-slice | bytes 2097156 | tf_op jit(solution)/shard_map/while/body/jit(dynamic_update_index_in_dim)/dynamic_update_slice | solution.py:87
  131.0 0.7 dynamic_slice.44
  132.3 0.1 dynamic_slice.46
  132.4 0.1 dynamic_slice.45
  132.5 3.6 fusion.51
  136.1 0.8 fusion.52
  136.9 1.1 copy-done.3
  138.0 1.8 fusion.53
  139.8 1.1 copy.23
  140.9 19.4 %dynamic_update_slice.5 = f32[2,512,512]{1,0,2:T(2,128)} dynamic-update-slice(f32[2,512,512]{1,0,2:T(2,128)} %get-tuple-element.145, f32[1,512,512]{1,0,2:T(1,128)S(1)} %copy.23, s32[]{:T(128)} %get-tuple-element.144, s32[]{:T(128)} %constant.16.clone.1..sunk, s32[]{:T(128)} %constant.16.clone.1..sunk) | dynamic-update-slice | bytes 2097156 | tf_op jit(solution)/shard_map/while/body/jit(dynamic_update_index_in_dim)/dynamic_update_slice | solution.py:87
  160.3 2.1 copy.21
  162.3 35.8 %all-reduce.3.cloned.1.call-done = (f32[1,512,512]{2,1,0:T(8,128)}, f32[1,512,512]{2,1,0:T(8,128)}, f32[1,512,512]{2,1,0:T(8,128)}) async-done(((f32[1,512,512]{2,1,0:T(8,128)}, f32[1,512,512]{2,1,0:T(8,128)}, f32[1,512,512]{2,1,0:T(8,128)}), (f32[1,512,512]{2,1,0:T(8,128)}, f32[1,512,512]{2,1,0:T(8,128)}, f32[1,512,512]{2,1,0:T(8,128)})) %all-reduce.3.cloned.1.call-update) | async-done | bytes 3145744 | tf_op jit(solution)/shard_map/psum | solution.py:109
  198.1 3.5 fusion.21
  201.6 5.2 %fusion.16 = bf16[1024,512]{0,1:T(8,128)(2,1)} fusion(f32[1024,512]{0,1:T(8,128)S(1)} %bitcast.81, f32[1024,512]{1,0:T(8,128)} %fusion.21, f32[1,512,512]{2,1,0:T(8,128)} %get-tuple-element.70, bf16[1,512,512]{2,1,0:T(8,128)(2,1)} %param.18, f32[1,512,512]{2,1,0:T(8,128)} %get-tuple-element.71, bf16[1,512,512]{2,1,0:T(8,128)(2,1)} %param.17, ...), kind=kOutput, calls=%fused_computation.27 | convolution fusion | flops 1081081856 | bytes 9441280 | tf_op jit(solution)/shard_map/htf,hfd->thd/dot_general | solution.py:116
  206.8 0.0 all-gather.3.cloned.1.call-update
  206.8 0.9 iota_reduce_fusion
  207.7 73.3 %all-gather.5.cloned.1.call-done = bf16[4096,512]{1,0:T(8,128)(2,1)} async-done(((bf16[128,512]{1,0:T(8,128)(2,1)}), bf16[4096,512]{1,0:T(8,128)(2,1)}) %all-gather.5.cloned.1.call-update) | async-done | bytes 4194320 | tf_op jit(solution)/shard_map/all_gather | solution.py:123
  281.0 51.2 %all-gather.3.cloned.1.call-done = bf16[1024,4096]{0,1:T(8,128)(2,1)} async-done(((bf16[1024,512]{0,1:T(8,128)(2,1)}), bf16[1024,4096]{0,1:T(8,128)(2,1)}) %all-gather.3.cloned.1.call-update) | async-done | bytes 8388624 | tf_op jit(solution)/shard_map/all_gather | solution.py:120
  332.2 9.1 %convolution_convert_fusion = bf16[1024,512]{1,0:T(8,128)(2,1)S(1)} fusion(bf16[1024,4096]{0,1:T(8,128)(2,1)} %all-gather.3.cloned.1.call-done, bf16[4096,512]{1,0:T(8,128)(2,1)} %all-gather.5.cloned.1.call-done), kind=kOutput, calls=%fused_computation.34 | convolution fusion | flops 4295491584 | bytes 13631488 | tf_op jit(solution)/shard_map/dot_general | solution.py:121
  341.2 0.6 gather_fusion
  341.9 38.6 %all_to_all.5 = bf16[32,32,512]{2,1,0:T(8,128)(2,1)S(1)} all-to-all(bf16[32,32,512]{2,1,0:T(8,128)(2,1)S(1)} %gather_fusion), channel_id=1, replica_groups=mesh['head'=8,'tok'=32] {'tok'}, dimensions={0} | all-to-all | bytes 2097152 | tf_op jit(solution)/shard_map/all_to_all | solution.py:133
  380.4 1.0 copy.35
  (22 shorter events, 0.1 us)
Async XLA Ops:
  6.5 191.6 %all-reduce.3.cloned.1.call-start = ((), (), s32[]{:S(2)}) async-start(), calls=%async_computation.3 | async-start | bytes 6291456 | tf_op jit(solution)/shard_map/psum | solution.py:109
  8.0 2.3 copy-start
  8.1 2.3 copy-start.5
  10.3 0.8 copy-start.6
  10.3 1.2 copy-start.1
  10.4 1.4 copy-start.4
  19.0 262.0 %all-gather.5.cloned.1.call-start = ((), (), s32[]{:S(2)}) async-start(), calls=%async_computation.2 | async-start | bytes 4325376 | tf_op jit(solution)/shard_map/all_gather | solution.py:123
  19.7 312.4 %all-gather.3.cloned.1.call-start = ((), (), s32[]{:S(2)}) async-start(), calls=%async_computation.1 | async-start | bytes 9437184 | tf_op jit(solution)/shard_map/all_gather | solution.py:120
  19.8 8.9 %copy-start.7 = (s32[64]{0:T(128)S(1)}, s32[64]{0:T(128)}, u32[]{:S(2)}) copy-start(s32[64]{0:T(128)} %param.20) | copy-start | bytes 772
  19.8 9.5 %copy-start.2 = (bf16[1024,512]{1,0:T(8,128)(2,1)S(1)}, bf16[1024,512]{1,0:T(8,128)(2,1)}, u32[]{:S(2)}) copy-start(bf16[1024,512]{1,0:T(8,128)(2,1)} %param.12) | copy-start | bytes 3145732
  21.3 69.6 %collective-permute-start = (bf16[2,1024,512]{2,1,0:T(8,128)(2,1)}, bf16[2,1024,512]{2,1,0:T(8,128)(2,1)}, u32[]{:S(2)}, u32[]{:S(2)}) collective-permute-start(bf16[2,1024,512]{2,1,0:T(8,128)(2,1)} %pad_maximum_fusion.1), channel_id=1, source_target_pairs={{0,1},{1,2},{2,3},{3,4},{4,5},{5,6},{6,7},{7,8},{8,9},{9,10},{10,1... | collective-permute-start | bytes 6291464 | tf_op jit(solution)/shard_map/ppermute | solution.py:14
  25.2 69.9 %collective-permute-start.1 = (bf16[2,1024,512]{2,1,0:T(8,128)(2,1)}, bf16[2,1024,512]{2,1,0:T(8,128)(2,1)}, u32[]{:S(2)}, u32[]{:S(2)}) collective-permute-start(bf16[2,1024,512]{2,1,0:T(8,128)(2,1)} %pad_maximum_fusion.1), channel_id=1, source_target_pairs={{1,0},{2,1},{3,2},{4,3},{5,4},{6,5},{7,6},{8,7},{9,8},{10,9},{11,1... | collective-permute-start | bytes 6291464 | tf_op jit(solution)/shard_map/ppermute | solution.py:14
  106.8 1.9 copy-start.3
  136.1 1.9 copy-start.3
  201.6 5.2 %copy-start.8 = (s32[1,32]{1,0:T(1,128)S(1)}, s32[1,32]{1,0:T(1,128)}, u32[]{:S(2)}) copy-start(s32[1,32]{1,0:T(1,128)} %param.21) | copy-start | bytes 388
Sparse Core Ops, SparseCore 0:
  19.1 178.9 all-reduce.2
  200.7 80.2 all-gather.4
  282.8 49.2 all-gather.2
where the time goes:
time: 391 us; the launch traced here: 388 us
  waiting for transfers between devices  226 us (58%)
  local copies, waits for them, and re-layouts  52.1 us (13%)
  matrix products  38.8 us (10%)
  blocking collectives  38.6 us (10%)
  between operations  13.4 us (3%)
  other arithmetic  9.8 us (3%)
  starting transfers between devices  7.41 us (2%)
    all_gather x1, waiting for transfers between devices, local(): lax.all_gather(out_proj, 'tok', axis=0, tiled=True)  73.3 us
    ppermute x2, waiting for transfers between devices, from_behind(): lax.ppermute(value, axis, [(source, source + steps) for source in range(l...  65.5 us
    all_gather x1, waiting for transfers between devices, local(): mixed_full = lax.all_gather(mixed, 'head', axis=1, tiled=True)  51.2 us
    dynamic_update_slice x4, local copies, waits for them, and re-layouts, local(): lax.map(attend, jnp.arange(n_blocks, dtype=jnp.int32))  41 us
    all_to_all x1, blocking collectives, local(): lax.all_to_all(outgoing, 'tok', split_axis=0, concat_axis=0, tiled=True)  38.6 us
    psum x1, waiting for transfers between devices, local(): lax.psum((grad_one, grad_three, grad_two), 'tok')  35.8 us
    dot_general x1, matrix products, local(): jnp.dot(mixed_full, lax.all_gather(out_proj, 'tok', axis=0, tiled=True),...  9.08 us
  transfers between devices with their start and end apart: 5, of which 5 were waited for; matrix products, arithmetic and copies ran while one was open for 19% of the time, Pallas kernels for 0%

commit v1 on v0

--- a/solution.py
+++ b/solution.py
@@ -117,7 +117,10 @@
         "htf,hfd->thd", hidden_q, new_two, preferred_element_type=jnp.float32
     ).reshape(tok_dev, local_width)
     mixed = (attended + fast_out).astype(jnp.bfloat16)
-    mixed_full = lax.all_gather(mixed, "head", axis=1, tiled=True)
+    mixed_full = jnp.concatenate(
+        lax.all_to_all(jnp.stack([mixed for _ in range(lax.axis_size("head"))]), "head", 0, 0),
+        axis=1,
+    )
     projected = jnp.dot(
         mixed_full,
         lax.all_gather(out_proj, "tok", axis=0, tiled=True),

time: 391 us -> 368 us (0.941)
  waiting for transfers between devices: 226 us -> 195 us
  local copies, waits for them, and re-layouts: 52.1 us -> 57.4 us
  starting transfers between devices: 7.41 us -> 12.7 us
    all_gather x1 -> x0, waiting for transfers between devices: 51.2 us -> none  [local(): mixed_full = lax.all_gather(mixed, 'head', axis=1, tiled=True)]
    all_to_all x0 -> x1, waiting for transfers between devices: none -> 30.9 us  [local(): lax.all_to_all(jnp.stack([mixed for _ in range(lax.axis_size('head'))]),...]
    all_gather x1, waiting for transfers between devices: 73.3 us -> 62.8 us  [local(): lax.all_gather(out_proj, 'tok', axis=0, tiled=True)]
    another operation x1 -> x2, local copies, waits for them, and re-layouts: 0.1 us -> 5.61 us  [the longest x1 5.52 us: local(): jnp.stack([mixed for _ in range(lax.axis_size('head'))])]
    all_to_all x0 -> x1, starting transfers between devices: none -> 5.31 us  [local(): lax.all_to_all(jnp.stack([mixed for _ in range(lax.axis_size('head'))]),...]
  transfers between devices with their start and end apart: 5 -> 5, of which waited for: 5 -> 5; matrix products, arithmetic and copies ran while one was open for 19% -> 22% of each run, Pallas kernels for 0% -> 0%
where the time goes in v1:
time: 368 us; the launch traced here: 364 us
  waiting for transfers between devices  195 us (53%)
  local copies, waits for them, and re-layouts  57.4 us (16%)
  matrix products  38.8 us (11%)
  blocking collectives  35.6 us (10%)
  between operations  13.7 us (4%)
  starting transfers between devices  12.7 us (3%)
  other arithmetic  9.56 us (3%)
    ppermute x2, waiting for transfers between devices, from_behind(): lax.ppermute(value, axis, [(source, source + steps) for source in range(l...  65.4 us
    all_gather x1, waiting for transfers between devices, local(): lax.all_gather(out_proj, 'tok', axis=0, tiled=True)  62.8 us
    dynamic_update_slice x4, local copies, waits for them, and re-layouts, local(): lax.map(attend, jnp.arange(n_blocks, dtype=jnp.int32))  41 us
    psum x1, waiting for transfers between devices, local(): lax.psum((grad_one, grad_three, grad_two), 'tok')  36.3 us
    all_to_all x1, blocking collectives, local(): lax.all_to_all(outgoing, 'tok', split_axis=0, concat_axis=0, tiled=True)  35.6 us
    all_to_all x1, waiting for transfers between devices, local(): lax.all_to_all(jnp.stack([mixed for _ in range(lax.axis_size('head'))]),...  30.9 us
    dot_general x1, matrix products, local(): jnp.dot(mixed_full, lax.all_gather(out_proj, 'tok', axis=0, tiled=True),...  9.09 us
  transfers between devices with their start and end apart: 5, of which 5 were waited for; matrix products, arithmetic and copies ran while one was open for 22% of the time, Pallas kernels for 0%

profile of v1, /device:TPU:32, one launch (start us, length us, event | category | flops | bytes accessed | tf_op | source)
XLA Modules:
  0.0 364.4 jit_solution(6910458415063587635)
XLA Ops:
  6.5 0.0 all-reduce.3.cloned.1.call-start
  6.5 1.5 fusion.12
  8.0 0.0 copy-start
  8.1 0.0 copy-start.5
  8.1 2.2 fusion.30
  10.3 0.0 copy-start.6
  10.3 0.0 copy-start.1
  10.4 0.0 copy-start.4
  10.4 0.8 fusion.28
  11.2 0.4 copy-done.1
  11.6 0.1 copy-done.4
  11.7 0.8 fusion.26
  12.5 2.1 convolution_bitcast_fusion
  14.6 2.3 convolution_bitcast_fusion.1
  16.9 2.1 convolution_bitcast_fusion.2
  19.0 0.0 all-reduce.3.cloned.1.call-update
  19.0 0.0 all-gather.2.cloned.1.call-start
  19.1 0.0 copy-start.7
  19.1 0.0 copy-start.2
  19.1 1.5 pad_maximum_fusion.1
  20.6 3.8 %collective-permute-start = (bf16[2,1024,512]{2,1,0:T(8,128)(2,1)}, bf16[2,1024,512]{2,1,0:T(8,128)(2,1)}, u32[]{:S(2)}, u32[]{:S(2)}) collective-permute-start(bf16[2,1024,512]{2,1,0:T(8,128)(2,1)} %pad_maximum_fusion.1), channel_id=1, source_target_pairs={{0,1},{1,2},{2,3},{3,4},{4,5},{5,6},{6,7},{7,8},{8,9},{9,10},{10,1... | collective-permute-start | bytes 6291464 | tf_op jit(solution)/shard_map/ppermute | solution.py:14
  24.4 3.5 collective-permute-start.1
  28.0 0.0 all-gather.2.cloned.1.call-update
  28.0 0.1 copy.16
  28.1 0.1 reduce-window.8
  28.2 0.1 multiply_reduce_fusion
  28.3 0.2 convert_reduce_fusion.1
  28.6 0.3 fusion.14
  28.9 61.3 %collective-permute-done = bf16[2,1024,512]{2,1,0:T(8,128)(2,1)} collective-permute-done((bf16[2,1024,512]{2,1,0:T(8,128)(2,1)}, bf16[2,1024,512]{2,1,0:T(8,128)(2,1)}, u32[]{:S(2)}, u32[]{:S(2)}) %collective-permute-start) | collective-permute-done | bytes 2097184 | tf_op jit(solution)/shard_map/ppermute | solution.py:14
  90.2 4.1 %collective-permute-done.1 = bf16[2,1024,512]{2,1,0:T(8,128)(2,1)} collective-permute-done((bf16[2,1024,512]{2,1,0:T(8,128)(2,1)}, bf16[2,1024,512]{2,1,0:T(8,128)(2,1)}, u32[]{:S(2)}, u32[]{:S(2)}) %collective-permute-start.1) | collective-permute-done | bytes 2097184 | tf_op jit(solution)/shard_map/ppermute | solution.py:14
  94.3 3.5 pad_maximum_fusion
  97.8 3.1 slice_bitcast_fusion
  100.9 58.2 %while.10 = (s32[]{:T(128)}, f32[2,512,512]{1,0,2:T(2,128)}, s32[2]{0:T(128)S(1)}, bf16[3072,1,512]{2,0,1:T(8,128)(2,1)}, s32[1024]{0:T(1024)S(1)}, /*index=5*/s...) while((s32[]{:T(128)}, f32[2,512,512]{1,0,2:T(2,128)}, ...), condition=%wide.region_7.8_spmd, body=%wide.region_4.7_spmd.sunk | while | flops 2696150016 | bytes 39371012 | solution.py:87
  100.9 0.6 dynamic_slice.44
  102.0 0.1 dynamic_slice.46
  102.1 0.1 dynamic_slice.45
  102.2 3.6 fusion.51
  105.8 0.8 fusion.52
  106.6 1.1 copy-done.3
  107.7 1.8 fusion.53
  109.5 1.1 copy.24
  110.6 19.4 %dynamic_update_slice.5 = f32[2,512,512]{1,0,2:T(2,128)} dynamic-update-slice(f32[2,512,512]{1,0,2:T(2,128)} %get-tuple-element.145, f32[1,512,512]{1,0,2:T(1,128)S(1)} %copy.24, s32[]{:T(128)} %get-tuple-element.144, s32[]{:T(128)} %constant.16.clone.1..sunk, s32[]{:T(128)} %constant.16.clone.1..sunk) | dynamic-update-slice | bytes 2097156 | tf_op jit(solution)/shard_map/while/body/jit(dynamic_update_index_in_dim)/dynamic_update_slice | solution.py:87
  130.0 0.6 dynamic_slice.44
  131.1 0.1 dynamic_slice.46
  131.2 0.1 dynamic_slice.45
  131.2 3.6 fusion.51
  134.9 0.8 fusion.52
  135.7 1.1 copy-done.3
  136.8 1.8 fusion.53
  138.6 1.1 copy.24
  139.6 19.4 %dynamic_update_slice.5 = f32[2,512,512]{1,0,2:T(2,128)} dynamic-update-slice(f32[2,512,512]{1,0,2:T(2,128)} %get-tuple-element.145, f32[1,512,512]{1,0,2:T(1,128)S(1)} %copy.24, s32[]{:T(128)} %get-tuple-element.144, s32[]{:T(128)} %constant.16.clone.1..sunk, s32[]{:T(128)} %constant.16.clone.1..sunk) | dynamic-update-slice | bytes 2097156 | tf_op jit(solution)/shard_map/while/body/jit(dynamic_update_index_in_dim)/dynamic_update_slice | solution.py:87
  159.1 2.1 copy.22
  161.1 36.3 %all-reduce.3.cloned.1.call-done = (f32[1,512,512]{2,1,0:T(8,128)}, f32[1,512,512]{2,1,0:T(8,128)}, f32[1,512,512]{2,1,0:T(8,128)}) async-done(((f32[1,512,512]{2,1,0:T(8,128)}, f32[1,512,512]{2,1,0:T(8,128)}, f32[1,512,512]{2,1,0:T(8,128)}), (f32[1,512,512]{2,1,0:T(8,128)}, f32[1,512,512]{2,1,0:T(8,128)}, f32[1,512,512]{2,1,0:T(8,128)})) %all-reduce.3.cloned.1.call-update) | async-done | bytes 3145744 | tf_op jit(solution)/shard_map/psum | solution.py:109
  197.4 3.5 fusion.21
  200.9 5.2 %fusion.16 = bf16[1024,512]{0,1:T(8,128)(2,1)} fusion(f32[1024,512]{0,1:T(8,128)S(1)} %bitcast.84, f32[1024,512]{1,0:T(8,128)} %fusion.21, f32[1,512,512]{2,1,0:T(8,128)} %get-tuple-element.70, bf16[1,512,512]{2,1,0:T(8,128)(2,1)} %param.18, f32[1,512,512]{2,1,0:T(8,128)} %get-tuple-element.71, bf16[1,512,512]{2,1,0:T(8,128)(2,1)} %param.17, ...), kind=kOutput, calls=%fused_computation.27 | convolution fusion | flops 1081081856 | bytes 9441280 | tf_op jit(solution)/shard_map/htf,hfd->thd/dot_general | solution.py:116
  206.0 5.5 %stack.11 = bf16[8,1024,512]{1,2,0:T(8,128)(2,1)} broadcast(bf16[1024,512]{0,1:T(8,128)(2,1)} %fusion.16), dimensions={1,2} | broadcast | bytes 9437184 | tf_op jit(solution)/shard_map/stack | solution.py:121
  211.5 5.3 %all-to-all-start = ((bf16[8,1024,512]{1,2,0:T(8,128)(2,1)}), bf16[8,1024,512]{1,2,0:T(8,128)(2,1)}, u32[]{:S(2)}, u32[]{:S(2)}) async-start(bf16[8,1024,512]{1,2,0:T(8,128)(2,1)} %stack.11), calls=%async_computation | async-start | bytes 16777216 | tf_op jit(solution)/shard_map/all_to_all | solution.py:121
  216.9 0.6 iota_reduce_fusion
  217.5 62.8 %all-gather.2.cloned.1.call-done = bf16[4096,512]{1,0:T(8,128)(2,1)} async-done(((bf16[128,512]{1,0:T(8,128)(2,1)}), bf16[4096,512]{1,0:T(8,128)(2,1)}) %all-gather.2.cloned.1.call-update) | async-done | bytes 4194320 | tf_op jit(solution)/shard_map/all_gather | solution.py:126
  280.3 30.9 %all-to-all-done = bf16[8,1024,512]{1,2,0:T(8,128)(2,1)} async-done(((bf16[8,1024,512]{1,2,0:T(8,128)(2,1)}), bf16[8,1024,512]{1,2,0:T(8,128)(2,1)}, u32[]{:S(2)}, u32[]{:S(2)}) %all-to-all-start) | async-done | bytes 8388640 | tf_op jit(solution)/shard_map/all_to_all | solution.py:121
  311.2 9.1 %convolution_convert_fusion = bf16[1024,512]{1,0:T(8,128)(2,1)S(1)} fusion(bf16[1024,4096]{0,1:T(8,128)(2,1)} %bitcast.25, bf16[4096,512]{1,0:T(8,128)(2,1)} %all-gather.2.cloned.1.call-done), kind=kOutput, calls=%fused_computation.34 | convolution fusion | flops 4295491584 | bytes 13631488 | tf_op jit(solution)/shard_map/dot_general | solution.py:124
  320.3 0.6 gather_fusion
  320.9 35.6 %all_to_all.10 = bf16[32,32,512]{2,1,0:T(8,128)(2,1)S(1)} all-to-all(bf16[32,32,512]{2,1,0:T(8,128)(2,1)S(1)} %gather_fusion), channel_id=1, replica_groups=mesh['head'=8,'tok'=32] {'tok'}, dimensions={0} | all-to-all | bytes 2097152 | tf_op jit(solution)/shard_map/all_to_all | solution.py:136
  356.6 1.0 copy.36
  (22 shorter events, 0.1 us)
Async XLA Ops:
  6.5 190.9 %all-reduce.3.cloned.1.call-start = ((), (), s32[]{:S(2)}) async-start(), calls=%async_computation.3 | async-start | bytes 6291456 | tf_op jit(solution)/shard_map/psum | solution.py:109
  8.0 2.3 copy-start
  8.1 2.3 copy-start.5
  10.3 0.8 copy-start.6
  10.3 1.2 copy-start.1
  10.4 1.4 copy-start.4
  19.0 261.3 %all-gather.2.cloned.1.call-start = ((), (), s32[]{:S(2)}) async-start(), calls=%async_computation.2 | async-start | bytes 4325376 | tf_op jit(solution)/shard_map/all_gather | solution.py:126
  19.1 9.0 %copy-start.7 = (s32[64]{0:T(128)S(1)}, s32[64]{0:T(128)}, u32[]{:S(2)}) copy-start(s32[64]{0:T(128)} %param.20) | copy-start | bytes 772
  19.1 9.5 %copy-start.2 = (bf16[1024,512]{1,0:T(8,128)(2,1)S(1)}, bf16[1024,512]{1,0:T(8,128)(2,1)}, u32[]{:S(2)}) copy-start(bf16[1024,512]{1,0:T(8,128)(2,1)} %param.12) | copy-start | bytes 3145732
  20.6 69.6 %collective-permute-start = (bf16[2,1024,512]{2,1,0:T(8,128)(2,1)}, bf16[2,1024,512]{2,1,0:T(8,128)(2,1)}, u32[]{:S(2)}, u32[]{:S(2)}) collective-permute-start(bf16[2,1024,512]{2,1,0:T(8,128)(2,1)} %pad_maximum_fusion.1), channel_id=1, source_target_pairs={{0,1},{1,2},{2,3},{3,4},{4,5},{5,6},{6,7},{7,8},{8,9},{9,10},{10,1... | collective-permute-start | bytes 6291464 | tf_op jit(solution)/shard_map/ppermute | solution.py:14
  24.4 69.8 %collective-permute-start.1 = (bf16[2,1024,512]{2,1,0:T(8,128)(2,1)}, bf16[2,1024,512]{2,1,0:T(8,128)(2,1)}, u32[]{:S(2)}, u32[]{:S(2)}) collective-permute-start(bf16[2,1024,512]{2,1,0:T(8,128)(2,1)} %pad_maximum_fusion.1), channel_id=1, source_target_pairs={{1,0},{2,1},{3,2},{4,3},{5,4},{6,5},{7,6},{8,7},{9,8},{10,9},{11,1... | collective-permute-start | bytes 6291464 | tf_op jit(solution)/shard_map/ppermute | solution.py:14
  105.8 1.9 copy-start.3
  134.9 1.9 copy-start.3
  211.5 5.3 %copy-start.8 = (s32[1,32]{1,0:T(1,128)S(1)}, s32[1,32]{1,0:T(1,128)}, u32[]{:S(2)}) copy-start(s32[1,32]{1,0:T(1,128)} %param.21) | copy-start | bytes 388
  211.5 99.7 %all-to-all-start = ((bf16[8,1024,512]{1,2,0:T(8,128)(2,1)}), bf16[8,1024,512]{1,2,0:T(8,128)(2,1)}, u32[]{:S(2)}, u32[]{:S(2)}) async-start(bf16[8,1024,512]{1,2,0:T(8,128)(2,1)} %stack.11), calls=%async_computation | async-start | bytes 16777216 | tf_op jit(solution)/shard_map/all_to_all | solution.py:121
Sparse Core Ops, SparseCore 0:
  19.1 178.2 all-reduce.2
  200.0 80.2 all-gather.1
